TPU v7x, 32 devices: a whole 2x2x4 slice. The times are simulated.
32 devices in a mesh: dp: 8 (over z, core), row: 2 (over x), col: 2 (over y).
Axes of the slice: x: 2, y: 2, z: 4, core: 2. Of those that a mesh axis runs over, the one named last changes fastest.
Arguments:
- tokens: bfloat16 [16384, 1024], P(('dp', 'row'), 'col'), may hold values from -6 to 6
- mixer_gain: float32 [1024], P('col'), may hold values from 0.1 to 1.9
- in_weight: bfloat16 [1024, 3, 1024], P('col', None, 'row'), may hold values from -0.1875 to 0.1875
- conv_kernel: float32 [3, 1024], P(None, 'row'), may hold values from -3.5 to 3.5
- out_weight: bfloat16 [1024, 1024], P('row', 'col'), may hold values from -0.1875 to 0.1875
- ffn_gain: float32 [1024], P('col'), may hold values from 0.1 to 1.9
- ffn_weight: bfloat16 [1024, 2, 4608], P('col', None, 'row'), may hold values from -0.1875 to 0.1875
- down_weight: bfloat16 [4608, 1024], P('row', 'col'), may hold values from -0.1875 to 0.1875
- cotangent: bfloat16 [16384, 1024], P(('dp', 'row'), 'col'), may hold values from -6 to 6
Outputs:
- output: bfloat16 [16384, 1024], P(('dp', 'row'), 'col')
- d_tokens: float32 [16384, 1024], P(('dp', 'row'), 'col')
- d_mixer_gain: float32 [1024], P('col')
- d_in_weight: float32 [1024, 3, 1024], P('col', None, 'row')
- d_conv_kernel: float32 [3, 1024], P(None, 'row')
- d_out_weight: float32 [1024, 1024], P('row', 'col')
- d_ffn_gain: float32 [1024], P('col')
- d_ffn_weight: float32 [1024, 2, 4608], P('col', None, 'row')
- d_down_weight: float32 [4608, 1024], P('row', 'col')
All inputs are finite; a program needn't handle non-finite values.
Results may differ from a plain program's by a relative error of at most 0.015.
Values may be sent and summed in bfloat16 or wider, within the bound.
No kernel may reach another device: no remote copies, remote signals or barrier semaphores. Data moves between devices by JAX's collectives and lax.ppermute only.
A program may use at most 320 MiB of HBM per device.

v0:
```python
import jax
import jax.numpy as jnp
from jax import lax
from jax.sharding import PartitionSpec as P

D = 1024
EPS = 1e-05


def shifted(block, axis, distance):
    devices = range(lax.axis_size(axis))
    route = [(i - distance, i) for i in devices if i - distance in devices]
    return lax.ppermute(block, axis, route)


def dense(left, matrix, transposed):
    if transposed:
        return lax.dot_general(
            left, matrix, (((1,), (1,)), ((), ())), preferred_element_type=jnp.float32
        )
    return jnp.dot(left, matrix, preferred_element_type=jnp.float32)


def grads_of(left, right):
    return lax.dot_general(
        left, right, (((0,), (0,)), ((), ())), preferred_element_type=jnp.float32
    )


def tokens_by_row(value):
    return lax.all_gather(value, "row", axis=0, tiled=True)


def tokens_by_col(value):
    return lax.all_gather(value, "col", axis=0, tiled=True)


def spread_wide(gathered, matrix, transposed):
    height = gathered.shape[0] // lax.axis_size("col")

    def partial_rows(start, count):
        return dense(gathered, matrix, transposed)

    return lax.psum_scatter(
        partial_rows(jnp.int32(0), height * lax.axis_size("col")),
        "col",
        scatter_dimension=0,
        tiled=True,
    )


def spread_narrow(gathered, matrix, transposed):
    height = gathered.shape[0] // lax.axis_size("row")

    def partial_rows(start, count):
        return dense(gathered, matrix, transposed)

    return lax.psum_scatter(
        partial_rows(jnp.int32(0), height * lax.axis_size("row")),
        "row",
        scatter_dimension=0,
        tiled=True,
    )


def width_total(value):
    return lax.psum(value, "col")


def local(
    tokens,
    mixer_gain,
    in_weight,
    conv_kernel,
    out_weight,
    ffn_gain,
    ffn_weight,
    down_weight,
    cotangent,
):
    xfloat = tokens.astype(jnp.float32)
    scale_one = lax.rsqrt(width_total(jnp.sum(xfloat * xfloat, axis=1, keepdims=True)) / D + EPS)
    normed_one = xfloat * scale_one
    hidden_one = (normed_one * mixer_gain).astype(jnp.bfloat16)
    wide_in = in_weight.reshape(in_weight.shape[0], -1)
    gathered_one = tokens_by_row(hidden_one)
    projected = spread_wide(gathered_one, wide_in, False)
    block_width = conv_kernel.shape[1]
    gate_b = projected[:, :block_width]
    gate_c = projected[:, block_width : 2 * block_width]
    values = projected[:, 2 * block_width :]
    mixed_in = gate_b * values
    previous = shifted(mixed_in[-2:], "col", 1)
    extended = jnp.concatenate([previous, mixed_in], 0)
    lag_one = extended[1:-1]
    lag_two = extended[:-2]
    convolved = conv_kernel[2] * mixed_in + conv_kernel[1] * lag_one + conv_kernel[0] * lag_two
    mixer_out = (gate_c * convolved).astype(jnp.bfloat16)
    gathered_mix = tokens_by_col(mixer_out)
    residual = xfloat + spread_narrow(gathered_mix, out_weight, False)
    scale_two = lax.rsqrt(
        width_total(jnp.sum(residual * residual, axis=1, keepdims=True)) / D + EPS
    )
    normed_two = residual * scale_two
    hidden_two = (normed_two * ffn_gain).astype(jnp.bfloat16)
    wide_ffn = ffn_weight.reshape(ffn_weight.shape[0], -1)
    gathered_two = tokens_by_row(hidden_two)
    gate_up = spread_wide(gathered_two, wide_ffn, False)
    inner_width = down_weight.shape[0]
    gate_part = gate_up[:, :inner_width]
    up_part = gate_up[:, inner_width:]
    sigmoid_gate = jax.nn.sigmoid(gate_part)
    activated = (gate_part * sigmoid_gate * up_part).astype(jnp.bfloat16)
    gathered_act = tokens_by_col(activated)
    output = (residual + spread_narrow(gathered_act, down_weight, False)).astype(jnp.bfloat16)
    cot_rows = tokens_by_row(cotangent)
    d_act = spread_wide(cot_rows, down_weight, True)
    grad_down = grads_of(gathered_act, cot_rows)
    d_gate = d_act * up_part * sigmoid_gate * (1.0 + gate_part * (1.0 - sigmoid_gate))
    d_up = d_act * gate_part * sigmoid_gate
    d_gate_up = jnp.concatenate([d_gate, d_up], 1).astype(jnp.bfloat16)
    dgu_rows = tokens_by_col(d_gate_up)
    d_hidden_two = spread_narrow(dgu_rows, wide_ffn, True)
    grad_ffn = grads_of(gathered_two, dgu_rows).reshape(ffn_weight.shape)
    scaled_two = d_hidden_two * ffn_gain
    inner_two = width_total(jnp.sum(scaled_two * normed_two, axis=1, keepdims=True)) / D
    d_residual = cotangent.astype(jnp.float32) + scale_two * (scaled_two - normed_two * inner_two)
    gain_two_part = jnp.sum(d_hidden_two * normed_two, axis=0)
    d_residual_b = d_residual.astype(jnp.bfloat16)
    dres_rows = tokens_by_row(d_residual_b)
    d_mix = spread_wide(dres_rows, out_weight, True)
    grad_out = grads_of(gathered_mix, dres_rows)
    d_gate_c = d_mix * convolved
    d_conv = d_mix * gate_c
    following = shifted(d_conv[:2], "col", -1)
    ahead_rows = jnp.concatenate([d_conv, following], 0)
    d_mixed = (
        conv_kernel[2] * d_conv
        + conv_kernel[1] * ahead_rows[1:-1]
        + conv_kernel[0] * ahead_rows[2:]
    )
    kernel_part = jnp.stack(
        [
            jnp.sum(d_conv * lag_two, axis=0),
            jnp.sum(d_conv * lag_one, axis=0),
            jnp.sum(d_conv * mixed_in, axis=0),
        ]
    )
    d_projected = jnp.concatenate([d_mixed * values, d_gate_c, d_mixed * gate_b], 1).astype(
        jnp.bfloat16
    )
    dproj_rows = tokens_by_col(d_projected)
    d_hidden_one = spread_narrow(dproj_rows, wide_in, True)
    grad_in = grads_of(gathered_one, dproj_rows).reshape(in_weight.shape)
    scaled_one = d_hidden_one * mixer_gain
    inner_one = width_total(jnp.sum(scaled_one * normed_one, axis=1, keepdims=True)) / D
    d_tokens = d_residual + scale_one * (scaled_one - normed_one * inner_one)
    gain_one_part = jnp.sum(d_hidden_one * normed_one, axis=0)
    grad_in, grad_out, grad_ffn, grad_down = (
        lax.psum(grad_in.astype(jnp.bfloat16), "dp").astype(jnp.float32),
        lax.psum(grad_out.astype(jnp.bfloat16), "dp").astype(jnp.float32),
        lax.psum(grad_ffn.astype(jnp.bfloat16), "dp").astype(jnp.float32),
        lax.psum(grad_down.astype(jnp.bfloat16), "dp").astype(jnp.float32),
    )
    gain_width = mixer_gain.shape[0]
    col_offset = lax.axis_index("col") * gain_width
    row_offset = lax.axis_index("row") * block_width
    zero_index = jnp.zeros((), jnp.int32)
    full_one = lax.dynamic_update_slice(jnp.zeros((D,), jnp.float32), gain_one_part, (col_offset,))
    full_two = lax.dynamic_update_slice(jnp.zeros((D,), jnp.float32), gain_two_part, (col_offset,))
    full_kernel = lax.dynamic_update_slice(
        jnp.zeros((3, D), jnp.float32), kernel_part, (zero_index, row_offset)
    )
    total_one, total_two, total_kernel = lax.psum(
        (full_one, full_two, full_kernel), ("dp", "row", "col")
    )
    grad_gain_one = lax.dynamic_slice_in_dim(total_one, col_offset, gain_width, 0)
    grad_gain_two = lax.dynamic_slice_in_dim(total_two, col_offset, gain_width, 0)
    grad_kernel = lax.dynamic_slice_in_dim(total_kernel, row_offset, block_width, 1)
    return (
        output,
        d_tokens,
        grad_gain_one,
        grad_in,
        grad_kernel,
        grad_out,
        grad_gain_two,
        grad_ffn,
        grad_down,
    )


def solution(mesh):
    in_specs = (
        P(("dp", "row"), "col"),
        P("col"),
        P("col", None, "row"),
        P(None, "row"),
        P("row", "col"),
        P("col"),
        P("col", None, "row"),
        P("row", "col"),
        P(("dp", "row"), "col"),
    )
    out_specs = (
        P(("dp", "row"), "col"),
        P(("dp", "row"), "col"),
        P("col"),
        P("col", None, "row"),
        P(None, "row"),
        P("row", "col"),
        P("col"),
        P("col", None, "row"),
        P("row", "col"),
    )
    return jax.shard_map(local, mesh=mesh, in_specs=in_specs, out_specs=out_specs, check_vma=False)
```

profile of v0, /device:TPU:0, one launch (start us, length us, event | category | flops | bytes accessed | tf_op | source)
XLA Modules:
  0.0 1960.4 jit_solution(6422226700840039610)
XLA Ops:
  8.9 5.9 psum.77
  20.6 32.4 %all-gather.9.cloned.1.call-done = bf16[2048,512]{1,0:T(8,128)(2,1)} async-done(((bf16[1024,512]{1,0:T(8,128)(2,1)}), bf16[2048,512]{1,0:T(8,128)(2,1)}) %all-gather.9.cloned.1.call-update) | async-done | bytes 2097168 | tf_op jit(solution)/shard_map/all_gather | solution.py:31
  52.9 10.0 fusion.20
  63.1 144.6 %reduce-scatter.9.cloned.1.call-done = f32[1024,1536]{1,0:T(8,128)} async-done(((f32[2048,1536]{1,0:T(8,128)}), f32[1024,1536]{1,0:T(8,128)}) %reduce-scatter.9.cloned.1.call-update) | async-done | bytes 6291472 | tf_op jit(solution)/shard_map/reduce_scatter | solution.py:44
  214.0 4.1 multiply_convert_fusion.7
  218.1 35.1 %all-gather.11.cloned.1.call-done = bf16[2048,512]{1,0:T(8,128)(2,1)} async-done(((bf16[1024,512]{1,0:T(8,128)(2,1)}), bf16[2048,512]{1,0:T(8,128)(2,1)}) %all-gather.11.cloned.1.call-update) | async-done | bytes 2097168 | tf_op jit(solution)/shard_map/all_gather | solution.py:35
  253.3 4.9 fusion.21
  258.8 53.9 %reduce-scatter.11.cloned.1.call-done = f32[1024,512]{1,0:T(8,128)} async-done(((f32[2048,512]{1,0:T(8,128)}), f32[1024,512]{1,0:T(8,128)}) %reduce-scatter.11.cloned.1.call-update) | async-done | bytes 2097168 | tf_op jit(solution)/shard_map/reduce_scatter | solution.py:58
  312.7 3.2 multiply_reduce_fusion.5
  315.9 4.9 psum.78
  320.9 3.0 multiply_convert_fusion.6
  324.0 23.2 %all-gather.17.cloned.1.call-done = bf16[2048,512]{1,0:T(8,128)(2,1)} async-done(((bf16[1024,512]{1,0:T(8,128)(2,1)}), bf16[2048,512]{1,0:T(8,128)(2,1)}) %all-gather.17.cloned.1.call-update) | async-done | bytes 2097168 | tf_op jit(solution)/shard_map/all_gather | solution.py:31
  347.2 11.5 fusion.24
  359.3 5.3 copy.22
  364.6 17.7 all-gather.13.cloned.1.call-done
  382.3 20.5 %fusion.22 = f32[2048,4608]{1,0:T(8,128)} fusion(bf16[2048,512]{1,0:T(8,128)(2,1)} %all-gather.13.cloned.1.call-done, bf16[512,4608]{1,0:T(8,128)(2,1)} %bitcast.44), kind=kOutput, calls=%fused_computation.62 | convolution fusion | flops 9663676416 | bytes 44564480 | tf_op jit(solution)/shard_map/dot_general | solution.py:21
  402.9 193.5 %reduce-scatter.17.cloned.1.call-done = f32[1024,2304]{1,0:T(8,128)} async-done(((f32[2048,2304]{1,0:T(8,128)}), f32[1024,2304]{1,0:T(8,128)}) %reduce-scatter.17.cloned.1.call-update) | async-done | bytes 9437200 | tf_op jit(solution)/shard_map/reduce_scatter | solution.py:44
  596.4 416.3 %reduce-scatter.13.cloned.1.call-done = f32[1024,4608]{1,0:T(8,128)} async-done(((f32[2048,4608]{1,0:T(8,128)}), f32[1024,4608]{1,0:T(8,128)}) %reduce-scatter.13.cloned.1.call-update) | async-done | bytes 18874384 | tf_op jit(solution)/shard_map/reduce_scatter | solution.py:44
  1012.7 13.4 multiply_convert_fusion.1
  1026.2 4.6 pad_maximum_fusion
  1030.8 224.4 %all-gather.19.cloned.1.call-done = bf16[2048,4608]{1,0:T(8,128)(2,1)} async-done(((bf16[1024,4608]{1,0:T(8,128)(2,1)}), bf16[2048,4608]{1,0:T(8,128)(2,1)}) %all-gather.19.cloned.1.call-update) | async-done | bytes 18874384 | tf_op jit(solution)/shard_map/all_gather | solution.py:35
  1255.2 16.5 fusion.25
  1271.8 54.5 %reduce-scatter.19.cloned.1.call-done = f32[1024,512]{1,0:T(8,128)} async-done(((f32[2048,512]{1,0:T(8,128)}), f32[1024,512]{1,0:T(8,128)}) %reduce-scatter.19.cloned.1.call-update) | async-done | bytes 2097168 | tf_op jit(solution)/shard_map/reduce_scatter | solution.py:58
  1329.1 4.9 psum.79
  1334.0 3.8 fusion.17
  1337.9 33.2 %all-gather.21.cloned.1.call-done = bf16[2048,512]{1,0:T(8,128)(2,1)} async-done(((bf16[1024,512]{1,0:T(8,128)(2,1)}), bf16[2048,512]{1,0:T(8,128)(2,1)}) %all-gather.21.cloned.1.call-update) | async-done | bytes 2097168 | tf_op jit(solution)/shard_map/all_gather | solution.py:31
  1371.1 5.0 fusion.26
  1376.9 53.7 %reduce-scatter.21.cloned.1.call-done = f32[1024,512]{1,0:T(8,128)} async-done(((f32[2048,512]{1,0:T(8,128)}), f32[1024,512]{1,0:T(8,128)}) %reduce-scatter.21.cloned.1.call-update) | async-done | bytes 2097168 | tf_op jit(solution)/shard_map/reduce_scatter | solution.py:44
  1430.6 5.3 multiply_reduce_fusion.3
  1437.4 4.0 collective-permute-done.1
  1448.3 101.9 %all-gather.15.cloned.1.call-done = bf16[2048,2304]{1,0:T(8,128)(2,1)} async-done(((bf16[1024,2304]{1,0:T(8,128)(2,1)}), bf16[2048,2304]{1,0:T(8,128)(2,1)}) %all-gather.15.cloned.1.call-update) | async-done | bytes 9437200 | tf_op jit(solution)/shard_map/all_gather | solution.py:35
  1550.2 10.5 convolution_convert_fusion.1
  1560.7 16.5 convolution_convert_fusion
  1577.2 7.2 convert_element_type.70
  1584.4 4.3 convolution_convert_fusion.3
  1588.7 43.9 %all-gather.23.cloned.1.call-done = bf16[2048,1536]{1,0:T(8,128)(2,1)} async-done(((bf16[1024,1536]{1,0:T(8,128)(2,1)}), bf16[2048,1536]{1,0:T(8,128)(2,1)}) %all-gather.23.cloned.1.call-update) | async-done | bytes 6291472 | tf_op jit(solution)/shard_map/all_gather | solution.py:35
  1632.5 8.0 convolution_convert_fusion.2
  1643.4 8.7 fusion.27
  1652.2 10.4 fusion.23
  1662.9 170.8 %all-reduce.4.cloned.1.call-done = (bf16[512,3,512]{0,2,1:T(8,128)(2,1)}, bf16[512,512]{1,0:T(8,128)(2,1)}, bf16[512,2,2304]{2,1,0:T(2,128)(2,1)}, bf16[2304,512]{1,0:T(8,128)(2,1)}) async-done(((bf16[512,3,512]{0,2,1:T(8,128)(2,1)}, bf16[512,512]{1,0:T(8,128)(2,1)}, bf16[512,2,2304]{2,1,0:T(2,128)(2,1)}, bf16[2304,512]{1,0:T(8,128)(2,1)}), (bf16[512,3,512]{0,2,1:T(8,128)(2,1)}, bf16[512,512]{1,0:T(8,128)(2,1)}, ...) | async-done | bytes 9175056 | tf_op jit(solution)/shard_map/psum | solution.py:160
  1833.7 7.4 convert_element_type.71
  1841.1 2.9 convert_element_type.73
  1844.0 3.2 copy.21
  1849.3 41.1 %reduce-scatter.23.cloned.1.call-done = f32[1024,512]{1,0:T(8,128)} async-done(((f32[2048,512]{1,0:T(8,128)}), f32[1024,512]{1,0:T(8,128)}) %reduce-scatter.23.cloned.1.call-update) | async-done | bytes 2097168 | tf_op jit(solution)/shard_map/reduce_scatter | solution.py:58
  1892.9 40.3 %all-reduce = (f32[1024]{0:T(1024)S(1)}, f32[3,1024]{1,0:T(4,128)S(1)}, f32[1024]{0:T(1024)S(1)}) all-reduce(f32[1024]{0:T(1024)S(1)} %dynamic_update_slice.9, f32[3,1024]{1,0:T(4,128)S(1)} %maximum_dynamic-update-slice_fusion, f32[1024]{0:T(1024)S(1)} %dynamic_update_slice.11), channel_id=1, replica_groups=mesh['dp'=8,'row'=2,'col'=2] {'dp','row','col'}, use_global_device_ids=true, to_apply=%region_17.0 | all-reduce | flops 5120 | bytes 40960 | tf_op jit(solution)/shard_map/psum | solution.py:174
  1934.6 5.1 psum.80
  1940.3 7.9 reduce-scatter.15.cloned.1.call-done
  1948.2 5.5 fusion.13
  (90 shorter events, 37.1 us)
Async XLA Ops:
  7.2 340.0 %copy-start = (bf16[2304,512]{1,0:T(8,128)(2,1)S(1)}, bf16[2304,512]{1,0:T(8,128)(2,1)}, u32[]{:S(2)}) copy-start(bf16[2304,512]{1,0:T(8,128)(2,1)} %param.16) | copy-start | bytes 7077892
  7.2 45.8 %all-gather.9.cloned.1.call-start = ((), (), s32[]{:S(2)}) async-start(), calls=%async_computation.8 | async-start | bytes 3145728 | tf_op jit(solution)/shard_map/all_gather | solution.py:31
  14.8 0.6 copy-start.7
  17.9 189.8 %reduce-scatter.9.cloned.1.call-start = ((), (), s32[]{:S(2)}) async-start(), calls=%async_computation.9 | async-start | bytes 18874368 | tf_op jit(solution)/shard_map/reduce_scatter | solution.py:44
  63.0 149.7 %copy-start.11 = (f32[3,512]{1,0:T(4,128)S(1)}, f32[3,512]{1,0:T(4,128)}, u32[]{:S(2)}) copy-start(f32[3,512]{1,0:T(4,128)} %param.12) | copy-start | bytes 18436
  63.0 190.3 %all-gather.11.cloned.1.call-start = ((), (), s32[]{:S(2)}) async-start(), calls=%async_computation.10 | async-start | bytes 3145728 | tf_op jit(solution)/shard_map/all_gather | solution.py:35
  210.4 7.7 copy-start.3
  210.4 3.6 collective-permute-start
  214.0 39.3 %copy-start.6 = (bf16[512,512]{1,0:T(8,128)(2,1)S(1)}, bf16[512,512]{1,0:T(8,128)(2,1)}, u32[]{:S(2)}) copy-start(bf16[512,512]{1,0:T(8,128)(2,1)} %param.13) | copy-start | bytes 1572868
  218.1 94.6 %reduce-scatter.11.cloned.1.call-start = ((), (), s32[]{:S(2)}) async-start(), calls=%async_computation.11 | async-start | bytes 6291456 | tf_op jit(solution)/shard_map/reduce_scatter | solution.py:58
  258.1 54.6 %copy-start.1 = (bf16[1024,512]{1,0:T(8,128)(2,1)S(1)}, bf16[1024,512]{1,0:T(8,128)(2,1)}, u32[]{:S(2)}) copy-start(bf16[1024,512]{1,0:T(8,128)(2,1)} %param.9) | copy-start | bytes 3145732
  258.2 89.0 %all-gather.17.cloned.1.call-start = ((), (), s32[]{:S(2)}) async-start(), calls=%async_computation.16 | async-start | bytes 3145728 | tf_op jit(solution)/shard_map/all_gather | solution.py:31
  258.7 62.1 %copy-start.9 = (f32[512]{0:T(512)S(1)}, f32[512]{0:T(512)}, u32[]{:S(2)}) copy-start(f32[512]{0:T(512)} %param.14) | copy-start | bytes 6148
  258.8 123.5 %all-gather.13.cloned.1.call-start = ((), (), s32[]{:S(2)}) async-start(), calls=%async_computation.12 | async-start | bytes 3145728 | tf_op jit(solution)/shard_map/all_gather | solution.py:31
  323.9 272.5 %reduce-scatter.17.cloned.1.call-start = ((), (), s32[]{:S(2)}) async-start(), calls=%async_computation.17 | async-start | bytes 28311552 | tf_op jit(solution)/shard_map/reduce_scatter | solution.py:44
  358.8 653.9 %reduce-scatter.13.cloned.1.call-start = ((), (), s32[]{:S(2)}) async-start(), calls=%async_computation.13 | async-start | bytes 56623104 | tf_op jit(solution)/shard_map/reduce_scatter | solution.py:44
  402.8 852.4 %all-gather.19.cloned.1.call-start = ((), (), s32[]{:S(2)}) async-start(), calls=%async_computation.18 | async-start | bytes 28311552 | tf_op jit(solution)/shard_map/all_gather | solution.py:35
  1030.7 295.5 %reduce-scatter.19.cloned.1.call-start = ((), (), s32[]{:S(2)}) async-start(), calls=%async_computation.19 | async-start | bytes 6291456 | tf_op jit(solution)/shard_map/reduce_scatter | solution.py:58
  1271.7 62.3 %copy-start.4 = (bf16[1024,512]{1,0:T(8,128)(2,1)S(1)}, bf16[1024,512]{1,0:T(8,128)(2,1)}, u32[]{:S(2)}) copy-start(bf16[1024,512]{1,0:T(8,128)(2,1)} %param.17) | copy-start | bytes 3145732
  1271.7 99.4 %all-gather.21.cloned.1.call-start = ((), (), s32[]{:S(2)}) async-start(), calls=%async_computation.20 | async-start | bytes 3145728 | tf_op jit(solution)/shard_map/all_gather | solution.py:31
  1337.8 92.8 %reduce-scatter.21.cloned.1.call-start = ((), (), s32[]{:S(2)}) async-start(), calls=%async_computation.21 | async-start | bytes 6291456 | tf_op jit(solution)/shard_map/reduce_scatter | solution.py:44
  1376.1 174.1 %all-gather.15.cloned.1.call-start = ((), (), s32[]{:S(2)}) async-start(), calls=%async_computation.14 | async-start | bytes 14155776 | tf_op jit(solution)/shard_map/all_gather | solution.py:35
  1376.8 255.7 %all-gather.23.cloned.1.call-start = ((), (), s32[]{:S(2)}) async-start(), calls=%async_computation.22 | async-start | bytes 9437184 | tf_op jit(solution)/shard_map/all_gather | solution.py:35
  1435.9 5.5 collective-permute-start.1
  1448.3 385.5 %all-reduce.4.cloned.1.call-start = ((), (), s32[]{:S(2)}) async-start(), calls=%async_computation.24 | async-start | bytes 18350080 | tf_op jit(solution)/shard_map/psum | solution.py:160
  1550.2 10.5 copy-start.12
  1643.2 247.2 %reduce-scatter.23.cloned.1.call-start = ((), (), s32[]{:S(2)}) async-start(), calls=%async_computation.23 | async-start | bytes 6291456 | tf_op jit(solution)/shard_map/reduce_scatter | solution.py:58
  1652.2 296.0 %reduce-scatter.15.cloned.1.call-start = ((), (), s32[]{:S(2)}) async-start(), calls=%async_computation.15 | async-start | bytes 6291456 | tf_op jit(solution)/shard_map/reduce_scatter | solution.py:58
  1833.7 7.4 copy-start.5
  1844.0 46.4 %copy-start.2 = (bf16[1024,512]{1,0:T(8,128)(2,1)S(1)}, bf16[1024,512]{1,0:T(8,128)(2,1)}, u32[]{:S(2)}) copy-start(bf16[1024,512]{1,0:T(8,128)(2,1)} %param.9) | copy-start | bytes 3145732
  1844.0 46.4 %copy-start.8 = (f32[1024,1]{0,1:T(1,128)S(1)}, f32[1024,1]{0,1:T(1,128)}, u32[]{:S(2)}) copy-start(f32[1024,1]{0,1:T(1,128)} %copy-done.7) | copy-start | bytes 12292
  1844.0 46.4 %copy-start.10 = (f32[512]{0:T(512)S(1)}, f32[512]{0:T(512)}, u32[]{:S(2)}) copy-start(f32[512]{0:T(512)} %param.10) | copy-start | bytes 6148
Sparse Core Ops, SparseCore 0:
  18.1 34.8 all-gather.8
  63.1 144.5 reduce-scatter.8
  218.2 35.0 all-gather.10
  258.3 54.3 reduce-scatter.10
  314.1 33.0 all-gather.16
  349.2 33.0 all-gather.12
  384.6 211.7 reduce-scatter.16
  598.7 413.9 reduce-scatter.12
  1030.9 224.3 all-gather.18
  1271.8 54.3 reduce-scatter.18
  1337.9 33.0 all-gather.20
  1376.2 54.3 reduce-scatter.20
  1432.2 117.9 all-gather.14
  1552.2 80.3 all-gather.22
  1643.3 190.3 all-reduce.3
  1835.9 54.4 reduce-scatter.22
  1892.6 55.5 reduce-scatter.14
where the time goes:
time: 1970 us; the launch traced here: 1960 us
  waiting for transfers between devices  1660 us (84%)
  matrix products  127 us (6%)
  other arithmetic  74.1 us (4%)
  blocking collectives  61.2 us (3%)
  local copies, waits for them, and re-layouts  23.9 us (1%)
    reduce_scatter x4, waiting for transfers between devices, spread_wide(): lax.psum_scatter(partial_rows(jnp.int32(0), height * lax.axis_size('col')...  808 us
    all_gather x4, waiting for transfers between devices, tokens_by_col(): return lax.all_gather(value, 'col', axis=0, tiled=True)  405 us
    psum x1, waiting for transfers between devices, local(): lax.psum(grad_in.astype(jnp.bfloat16), 'dp').astype(jnp.float32)  171 us
    reduce_scatter x4, waiting for transfers between devices, spread_narrow(): lax.psum_scatter(partial_rows(jnp.int32(0), height * lax.axis_size('row')...  157 us
    all_gather x4, waiting for transfers between devices, tokens_by_row(): return lax.all_gather(value, 'row', axis=0, tiled=True)  107 us
    dot_general x4, matrix products, dense(): return jnp.dot(left, matrix, preferred_element_type=jnp.float32)  45.8 us
    dot_general x4, matrix products, dense(): lax.dot_general(left, matrix, (((1,), (1,)), ((), ())), preferred_element...  41.7 us
    psum x1, blocking collectives, local(): lax.psum((full_one, full_two, full_kernel), ('dp', 'row', 'col'))  40.3 us
  transfers between devices with their start and end apart: 19, of which 19 were waited for; matrix products, arithmetic and copies ran while one was open for 7% of the time, Pallas kernels for 0%

commit v1 on v0

--- a/solution.py
+++ b/solution.py
@@ -5,6 +5,11 @@
 
 D = 1024
 EPS = 1e-05
+
+
+def summed_here(block, axis):
+    parts = lax.all_gather(block, axis)
+    return jnp.sum(parts, axis=0)
 
 
 def shifted(block, axis, distance):
@@ -157,7 +162,7 @@
     d_tokens = d_residual + scale_one * (scaled_one - normed_one * inner_one)
     gain_one_part = jnp.sum(d_hidden_one * normed_one, axis=0)
     grad_in, grad_out, grad_ffn, grad_down = (
-        lax.psum(grad_in.astype(jnp.bfloat16), "dp").astype(jnp.float32),
+        summed_here(grad_in.astype(jnp.bfloat16), "dp").astype(jnp.float32),
         lax.psum(grad_out.astype(jnp.bfloat16), "dp").astype(jnp.float32),
         lax.psum(grad_ffn.astype(jnp.bfloat16), "dp").astype(jnp.float32),
         lax.psum(grad_down.astype(jnp.bfloat16), "dp").astype(jnp.float32),

time: 1970 us -> 2060 us (1.046)
  waiting for transfers between devices: 1660 us -> 1730 us
    all_gather x0 -> x1, waiting for transfers between devices: none -> 113 us  [summed_here(): parts = lax.all_gather(block, axis)]
    psum x1, waiting for transfers between devices: 171 us -> 131 us  [local(): lax.psum(grad_out.astype(jnp.bfloat16), 'dp').astype(jnp.float32)]
  transfers between devices with their start and end apart: 19 -> 20, of which waited for: 19 -> 20; matrix products, arithmetic and copies ran while one was open for 7% -> 7% of each run, Pallas kernels for 0% -> 0%
where the time goes in v1:
time: 2060 us; the launch traced here: 2050 us
  waiting for transfers between devices  1730 us (84%)
  matrix products  127 us (6%)
  other arithmetic  80.9 us (4%)
  blocking collectives  61.5 us (3%)
  local copies, waits for them, and re-layouts  29 us (1%)
    reduce_scatter x4, waiting for transfers between devices, spread_wide(): lax.psum_scatter(partial_rows(jnp.int32(0), height * lax.axis_size('col')...  808 us
    all_gather x4, waiting for transfers between devices, tokens_by_col(): return lax.all_gather(value, 'col', axis=0, tiled=True)  405 us
    reduce_scatter x4, waiting for transfers between devices, spread_narrow(): lax.psum_scatter(partial_rows(jnp.int32(0), height * lax.axis_size('row')...  161 us
    psum x1, waiting for transfers between devices, local(): lax.psum(grad_out.astype(jnp.bfloat16), 'dp').astype(jnp.float32)  131 us
    all_gather x1, waiting for transfers between devices, summed_here(): parts = lax.all_gather(block, axis)  113 us
    all_gather x4, waiting for transfers between devices, tokens_by_row(): return lax.all_gather(value, 'row', axis=0, tiled=True)  107 us
    dot_general x4, matrix products, dense(): return jnp.dot(left, matrix, preferred_element_type=jnp.float32)  45.9 us
    dot_general x4, matrix products, dense(): lax.dot_general(left, matrix, (((1,), (1,)), ((), ())), preferred_element...  41.7 us
  transfers between devices with their start and end apart: 20, of which 20 were waited for; matrix products, arithmetic and copies ran while one was open for 7% of the time, Pallas kernels for 0%

profile of v1, /device:TPU:0, one launch (start us, length us, event | category | flops | bytes accessed | tf_op | source)
XLA Modules:
  0.0 2049.5 jit_solution(395635068826477682)
XLA Ops:
  8.9 5.9 psum.70
  20.6 32.4 %all-gather.10.cloned.1.call-done = bf16[2048,512]{1,0:T(8,128)(2,1)} async-done(((bf16[1024,512]{1,0:T(8,128)(2,1)}), bf16[2048,512]{1,0:T(8,128)(2,1)}) %all-gather.10.cloned.1.call-update) | async-done | bytes 2097168 | tf_op jit(solution)/shard_map/all_gather | solution.py:36
  52.9 10.0 fusion.20
  63.1 144.6 %reduce-scatter.9.cloned.1.call-done = f32[1024,1536]{1,0:T(8,128)} async-done(((f32[2048,1536]{1,0:T(8,128)}), f32[1024,1536]{1,0:T(8,128)}) %reduce-scatter.9.cloned.1.call-update) | async-done | bytes 6291472 | tf_op jit(solution)/shard_map/reduce_scatter | solution.py:49
  214.0 4.1 multiply_convert_fusion.7
  218.2 35.1 %all-gather.12.cloned.1.call-done = bf16[2048,512]{1,0:T(8,128)(2,1)} async-done(((bf16[1024,512]{1,0:T(8,128)(2,1)}), bf16[2048,512]{1,0:T(8,128)(2,1)}) %all-gather.12.cloned.1.call-update) | async-done | bytes 2097168 | tf_op jit(solution)/shard_map/all_gather | solution.py:40
  253.3 4.8 fusion.21
  258.8 53.9 %reduce-scatter.11.cloned.1.call-done = f32[1024,512]{1,0:T(8,128)} async-done(((f32[2048,512]{1,0:T(8,128)}), f32[1024,512]{1,0:T(8,128)}) %reduce-scatter.11.cloned.1.call-update) | async-done | bytes 2097168 | tf_op jit(solution)/shard_map/reduce_scatter | solution.py:63
  312.7 3.3 multiply_reduce_fusion.5
  316.0 4.9 psum.71
  324.0 23.2 %all-gather.18.cloned.1.call-done = bf16[2048,512]{1,0:T(8,128)(2,1)} async-done(((bf16[1024,512]{1,0:T(8,128)(2,1)}), bf16[2048,512]{1,0:T(8,128)(2,1)}) %all-gather.18.cloned.1.call-update) | async-done | bytes 2097168 | tf_op jit(solution)/shard_map/all_gather | solution.py:36
  347.2 11.5 fusion.24
  359.0 5.3 copy.26
  364.3 18.0 all-gather.14.cloned.1.call-done
  382.3 20.5 fusion.22
  402.9 193.5 %reduce-scatter.17.cloned.1.call-done = f32[1024,2304]{1,0:T(8,128)} async-done(((f32[2048,2304]{1,0:T(8,128)}), f32[1024,2304]{1,0:T(8,128)}) %reduce-scatter.17.cloned.1.call-update) | async-done | bytes 9437200 | tf_op jit(solution)/shard_map/reduce_scatter | solution.py:49
  596.4 416.3 %reduce-scatter.13.cloned.1.call-done = f32[1024,4608]{1,0:T(8,128)} async-done(((f32[2048,4608]{1,0:T(8,128)}), f32[1024,4608]{1,0:T(8,128)}) %reduce-scatter.13.cloned.1.call-update) | async-done | bytes 18874384 | tf_op jit(solution)/shard_map/reduce_scatter | solution.py:49
  1012.7 13.4 multiply_convert_fusion.1
  1026.2 4.6 pad_maximum_fusion
  1030.8 224.4 %all-gather.20.cloned.1.call-done = bf16[2048,4608]{1,0:T(8,128)(2,1)} async-done(((bf16[1024,4608]{1,0:T(8,128)(2,1)}), bf16[2048,4608]{1,0:T(8,128)(2,1)}) %all-gather.20.cloned.1.call-update) | async-done | bytes 18874384 | tf_op jit(solution)/shard_map/all_gather | solution.py:40
  1255.2 16.5 fusion.25
  1271.8 54.5 %reduce-scatter.19.cloned.1.call-done = f32[1024,512]{1,0:T(8,128)} async-done(((f32[2048,512]{1,0:T(8,128)}), f32[1024,512]{1,0:T(8,128)}) %reduce-scatter.19.cloned.1.call-update) | async-done | bytes 2097168 | tf_op jit(solution)/shard_map/reduce_scatter | solution.py:63
  1329.1 4.9 psum.72
  1334.0 3.8 fusion.17
  1337.9 33.2 %all-gather.22.cloned.1.call-done = bf16[2048,512]{1,0:T(8,128)(2,1)} async-done(((bf16[1024,512]{1,0:T(8,128)(2,1)}), bf16[2048,512]{1,0:T(8,128)(2,1)}) %all-gather.22.cloned.1.call-update) | async-done | bytes 2097168 | tf_op jit(solution)/shard_map/all_gather | solution.py:36
  1371.1 5.0 fusion.26
  1376.9 53.7 %reduce-scatter.21.cloned.1.call-done = f32[1024,512]{1,0:T(8,128)} async-done(((f32[2048,512]{1,0:T(8,128)}), f32[1024,512]{1,0:T(8,128)}) %reduce-scatter.21.cloned.1.call-update) | async-done | bytes 2097168 | tf_op jit(solution)/shard_map/reduce_scatter | solution.py:49
  1430.6 5.2 multiply_reduce_fusion.3
  1437.3 4.0 collective-permute-done.1
  1448.2 101.9 %all-gather.16.cloned.1.call-done = bf16[2048,2304]{1,0:T(8,128)(2,1)} async-done(((bf16[1024,2304]{1,0:T(8,128)(2,1)}), bf16[2048,2304]{1,0:T(8,128)(2,1)}) %all-gather.16.cloned.1.call-update) | async-done | bytes 9437200 | tf_op jit(solution)/shard_map/all_gather | solution.py:40
  1550.2 10.6 convolution_convert_fusion.1
  1560.8 16.5 convolution_convert_fusion
  1577.2 7.2 convert_element_type.79
  1584.4 4.3 convolution_convert_fusion.3
  1589.2 43.4 %all-gather.24.cloned.1.call-done = bf16[2048,1536]{1,0:T(8,128)(2,1)} async-done(((bf16[1024,1536]{1,0:T(8,128)(2,1)}), bf16[2048,1536]{1,0:T(8,128)(2,1)}) %all-gather.24.cloned.1.call-update) | async-done | bytes 6291472 | tf_op jit(solution)/shard_map/all_gather | solution.py:40
  1632.5 8.7 fusion.27
  1641.4 10.5 fusion.23
  1651.9 8.1 convolution_convert_fusion.2
  1665.5 130.9 %all-reduce.4.cloned.1.call-done = (bf16[512,512]{1,0:T(8,128)(2,1)}, bf16[512,2,2304]{2,1,0:T(2,128)(2,1)}, bf16[2304,512]{1,0:T(8,128)(2,1)}) async-done(((bf16[512,512]{1,0:T(8,128)(2,1)}, bf16[512,2,2304]{2,1,0:T(2,128)(2,1)}, bf16[2304,512]{1,0:T(8,128)(2,1)}), (bf16[512,512]{1,0:T(8,128)(2,1)}, bf16[512,2,2304]{2,1,0:T(2,128)(2,1)}, bf16[2304,512]{1,0:T(8,128)(2,1)})) %all-reduce.4.cloned.1.call-update) | async-done | bytes 7602192 | tf_op jit(solution)/shard_map/psum | solution.py:166
  1796.4 7.4 convert_element_type.80
  1807.7 45.3 %reduce-scatter.23.cloned.1.call-done = f32[1024,512]{1,0:T(8,128)} async-done(((f32[2048,512]{1,0:T(8,128)}), f32[1024,512]{1,0:T(8,128)}) %reduce-scatter.23.cloned.1.call-update) | async-done | bytes 2097168 | tf_op jit(solution)/shard_map/reduce_scatter | solution.py:63
  1855.5 40.4 %all-reduce = (f32[1024]{0:T(1024)S(1)}, f32[3,1024]{1,0:T(4,128)S(1)}, f32[1024]{0:T(1024)S(1)}) all-reduce(f32[1024]{0:T(1024)S(1)} %dynamic_update_slice.9, f32[3,1024]{1,0:T(4,128)S(1)} %maximum_dynamic-update-slice_fusion, f32[1024]{0:T(1024)S(1)} %dynamic_update_slice.11), channel_id=1, replica_groups=mesh['dp'=8,'row'=2,'col'=2] {'dp','row','col'}, use_global_device_ids=true, to_apply=%region_17.0 | all-reduce | flops 5120 | bytes 40960 | tf_op jit(solution)/shard_map/psum | solution.py:179
  1897.3 5.3 psum.73
  1903.2 7.6 reduce-scatter.15.cloned.1.call-done
  1910.8 5.5 fusion.13
  1916.3 112.6 %all-gather.26.cloned.1.call-done = bf16[8,512,3,512]{3,1,2,0:T(8,128)(2,1)} async-done(((bf16[1,512,3,512]{3,1,2,0:T(8,128)(2,1)}), bf16[8,512,3,512]{3,1,2,0:T(8,128)(2,1)}) %all-gather.26.cloned.1.call-update) | async-done | bytes 12582928 | tf_op jit(solution)/shard_map/all_gather | solution.py:11
  2028.8 8.0 reduce_sum.98
  2039.4 3.1 copy.24
  (98 shorter events, 47.1 us)
Async XLA Ops:
  7.2 340.0 %copy-start = (bf16[2304,512]{1,0:T(8,128)(2,1)S(1)}, bf16[2304,512]{1,0:T(8,128)(2,1)}, u32[]{:S(2)}) copy-start(bf16[2304,512]{1,0:T(8,128)(2,1)} %param.16) | copy-start | bytes 7077892
  7.2 45.8 %all-gather.10.cloned.1.call-start = ((), (), s32[]{:S(2)}) async-start(), calls=%async_computation.8 | async-start | bytes 3145728 | tf_op jit(solution)/shard_map/all_gather | solution.py:36
  14.8 0.6 copy-start.8
  17.9 189.8 %reduce-scatter.9.cloned.1.call-start = ((), (), s32[]{:S(2)}) async-start(), calls=%async_computation.9 | async-start | bytes 18874368 | tf_op jit(solution)/shard_map/reduce_scatter | solution.py:49
  63.0 149.7 %copy-start.12 = (f32[3,512]{1,0:T(4,128)S(1)}, f32[3,512]{1,0:T(4,128)}, u32[]{:S(2)}) copy-start(f32[3,512]{1,0:T(4,128)} %param.12) | copy-start | bytes 18436
  63.0 190.3 %all-gather.12.cloned.1.call-start = ((), (), s32[]{:S(2)}) async-start(), calls=%async_computation.10 | async-start | bytes 3145728 | tf_op jit(solution)/shard_map/all_gather | solution.py:40
  210.4 7.7 copy-start.3
  210.4 3.6 collective-permute-start
  214.0 39.3 %copy-start.6 = (bf16[512,512]{1,0:T(8,128)(2,1)S(1)}, bf16[512,512]{1,0:T(8,128)(2,1)}, u32[]{:S(2)}) copy-start(bf16[512,512]{1,0:T(8,128)(2,1)} %param.13) | copy-start | bytes 1572868
  218.1 94.6 %reduce-scatter.11.cloned.1.call-start = ((), (), s32[]{:S(2)}) async-start(), calls=%async_computation.11 | async-start | bytes 6291456 | tf_op jit(solution)/shard_map/reduce_scatter | solution.py:63
  258.1 54.6 %copy-start.1 = (bf16[1024,512]{1,0:T(8,128)(2,1)S(1)}, bf16[1024,512]{1,0:T(8,128)(2,1)}, u32[]{:S(2)}) copy-start(bf16[1024,512]{1,0:T(8,128)(2,1)} %param.9) | copy-start | bytes 3145732
  258.2 89.1 %all-gather.18.cloned.1.call-start = ((), (), s32[]{:S(2)}) async-start(), calls=%async_computation.16 | async-start | bytes 3145728 | tf_op jit(solution)/shard_map/all_gather | solution.py:36
  258.7 62.1 %copy-start.10 = (f32[512]{0:T(512)S(1)}, f32[512]{0:T(512)}, u32[]{:S(2)}) copy-start(f32[512]{0:T(512)} %param.14) | copy-start | bytes 6148
  258.8 123.6 %all-gather.14.cloned.1.call-start = ((), (), s32[]{:S(2)}) async-start(), calls=%async_computation.12 | async-start | bytes 3145728 | tf_op jit(solution)/shard_map/all_gather | solution.py:36
  323.9 272.5 %reduce-scatter.17.cloned.1.call-start = ((), (), s32[]{:S(2)}) async-start(), calls=%async_computation.17 | async-start | bytes 28311552 | tf_op jit(solution)/shard_map/reduce_scatter | solution.py:49
  358.8 653.9 %reduce-scatter.13.cloned.1.call-start = ((), (), s32[]{:S(2)}) async-start(), calls=%async_computation.13 | async-start | bytes 56623104 | tf_op jit(solution)/shard_map/reduce_scatter | solution.py:49
  402.8 852.4 %all-gather.20.cloned.1.call-start = ((), (), s32[]{:S(2)}) async-start(), calls=%async_computation.18 | async-start | bytes 28311552 | tf_op jit(solution)/shard_map/all_gather | solution.py:40
  1030.7 295.5 %reduce-scatter.19.cloned.1.call-start = ((), (), s32[]{:S(2)}) async-start(), calls=%async_computation.19 | async-start | bytes 6291456 | tf_op jit(solution)/shard_map/reduce_scatter | solution.py:63
  1271.7 62.3 %copy-start.4 = (bf16[1024,512]{1,0:T(8,128)(2,1)S(1)}, bf16[1024,512]{1,0:T(8,128)(2,1)}, u32[]{:S(2)}) copy-start(bf16[1024,512]{1,0:T(8,128)(2,1)} %param.17) | copy-start | bytes 3145732
  1271.7 99.4 %all-gather.22.cloned.1.call-start = ((), (), s32[]{:S(2)}) async-start(), calls=%async_computation.20 | async-start | bytes 3145728 | tf_op jit(solution)/shard_map/all_gather | solution.py:36
  1337.8 92.8 %reduce-scatter.21.cloned.1.call-start = ((), (), s32[]{:S(2)}) async-start(), calls=%async_computation.21 | async-start | bytes 6291456 | tf_op jit(solution)/shard_map/reduce_scatter | solution.py:49
  1376.1 174.1 %all-gather.16.cloned.1.call-start = ((), (), s32[]{:S(2)}) async-start(), calls=%async_computation.14 | async-start | bytes 14155776 | tf_op jit(solution)/shard_map/all_gather | solution.py:40
  1376.8 255.7 %all-gather.24.cloned.1.call-start = ((), (), s32[]{:S(2)}) async-start(), calls=%async_computation.22 | async-start | bytes 9437184 | tf_op jit(solution)/shard_map/all_gather | solution.py:40
  1435.8 5.5 collective-permute-start.1
  1448.2 348.2 %all-reduce.4.cloned.1.call-start = ((), (), s32[]{:S(2)}) async-start(), calls=%async_computation.25 | async-start | bytes 15204352 | tf_op jit(solution)/shard_map/psum | solution.py:166
  1550.2 10.6 copy-start.13
  1588.7 264.3 %reduce-scatter.23.cloned.1.call-start = ((), (), s32[]{:S(2)}) async-start(), calls=%async_computation.23 | async-start | bytes 6291456 | tf_op jit(solution)/shard_map/reduce_scatter | solution.py:63
  1641.3 269.5 %reduce-scatter.15.cloned.1.call-start = ((), (), s32[]{:S(2)}) async-start(), calls=%async_computation.15 | async-start | bytes 6291456 | tf_op jit(solution)/shard_map/reduce_scatter | solution.py:63
  1651.9 377.0 %all-gather.26.cloned.1.call-start = ((), (), s32[]{:S(2)}) async-start(), calls=%async_computation.24 | async-start | bytes 14155776 | tf_op jit(solution)/shard_map/all_gather | solution.py:11
  1796.4 7.4 copy-start.5
  1803.7 2.9 copy-start.7
  1803.7 49.3 %copy-start.9 = (f32[1024,1]{0,1:T(1,128)S(1)}, f32[1024,1]{0,1:T(1,128)}, u32[]{:S(2)}) copy-start(f32[1024,1]{0,1:T(1,128)} %copy-done.8) | copy-start | bytes 12292
  1803.8 49.3 %copy-start.11 = (f32[512]{0:T(512)S(1)}, f32[512]{0:T(512)}, u32[]{:S(2)}) copy-start(f32[512]{0:T(512)} %param.10) | copy-start | bytes 6148
  1806.6 46.4 %copy-start.2 = (bf16[1024,512]{1,0:T(8,128)(2,1)S(1)}, bf16[1024,512]{1,0:T(8,128)(2,1)}, u32[]{:S(2)}) copy-start(bf16[1024,512]{1,0:T(8,128)(2,1)} %param.9) | copy-start | bytes 3145732
Sparse Core Ops, SparseCore 0:
  18.1 34.8 all-gather.9
  63.1 144.5 reduce-scatter.8
  218.2 35.0 all-gather.11
  258.3 54.3 reduce-scatter.10
  314.1 33.0 all-gather.17
  349.2 33.0 all-gather.13
  384.6 211.7 reduce-scatter.16
  598.7 413.9 reduce-scatter.12
  1030.9 224.3 all-gather.19
  1271.8 54.3 reduce-scatter.18
  1337.9 33.0 all-gather.21
  1376.2 54.3 reduce-scatter.20
  1432.2 117.9 all-gather.15
  1552.2 80.3 all-gather.23
  1635.6 160.7 all-reduce.3
  1798.5 54.4 reduce-scatter.22
  1855.1 55.5 reduce-scatter.14
  1912.3 116.5 all-gather.25
